TPU v7x, 32 devices: a whole 2x2x4 slice. The times are simulated.
32 devices in a mesh: dp: 8 (over y, x, core), mp: 4 (over z).
Axes of the slice: x: 2, y: 2, z: 4, core: 2. Of those that a mesh axis runs over, the one named last changes fastest.
Arguments:
- hidden: bfloat16 [4096, 768], P('dp'), may hold values from -6 to 6
- memory: bfloat16 [32768, 768], P('dp', 'mp'), may hold values from -6 to 6
- out_grad: bfloat16 [4096, 768], P('dp'), may hold values from -6 to 6
- dec_starts: int32 [32, 4], P('dp'), may hold values from 0 to 127, as said below
- dec_length: int32 [32], P('dp'), may hold values from 96 to 128
- mem_starts: int32 [32, 4], P('dp'), may hold values from 0 to 1023, as said below
- mem_length: int32 [32], P('dp'), may hold values from 768 to 1024
- self_qkv: bfloat16 [3, 768, 768], P(None, None, 'mp'), may hold values from -0.25 to 0.25
- self_qv_bias: float32 [2, 768], P(None, 'mp'), may hold values from -3 to 3
- self_proj: bfloat16 [768, 768], P('mp'), may hold values from -0.3125 to 0.3125
- cross_query: bfloat16 [768, 768], P(None, 'mp'), may hold values from -0.25 to 0.25
- cross_kv: bfloat16 [2, 768, 768], P(None, None, 'mp'), may hold values from -0.25 to 0.25
- cross_qv_bias: float32 [2, 768], P(None, 'mp'), may hold values from -3 to 3
- cross_proj: bfloat16 [768, 768], P('mp'), may hold values from -0.875 to 0.875
- ffn_in: bfloat16 [768, 3072], P(None, 'mp'), may hold values from -0.21875 to 0.21875
- ffn_in_bias: float32 [3072], P('mp'), may hold values from -3 to 3
- ffn_out: bfloat16 [3072, 768], P('mp'), may hold values from -0.15625 to 0.15625
- out_biases: float32 [3, 768], replicated, may hold values from -3 to 3
- norm_gains: float32 [3, 768], replicated, may hold values from 0.25 to 1.75
- norm_biases: float32 [3, 768], replicated, may hold values from -2 to 2
Outputs:
- result: bfloat16 [4096, 768], P('dp')
- hidden_grad: float32 [4096, 768], P('dp')
- memory_grad: float32 [32768, 768], P('dp', 'mp')
- self_qkv_grad: float32 [3, 768, 768], P(None, None, 'mp')
- self_qv_bias_grad: float32 [2, 768], P(None, 'mp')
- self_proj_grad: float32 [768, 768], P('mp')
- cross_query_grad: float32 [768, 768], P(None, 'mp')
- cross_kv_grad: float32 [2, 768, 768], P(None, None, 'mp')
- cross_qv_bias_grad: float32 [2, 768], P(None, 'mp')
- cross_proj_grad: float32 [768, 768], P('mp')
- ffn_in_grad: float32 [768, 3072], P(None, 'mp')
- ffn_in_bias_grad: float32 [3072], P('mp')
- ffn_out_grad: float32 [3072, 768], P('mp')
- out_biases_grad: float32 [3, 768], replicated
- norm_gains_grad: float32 [3, 768], replicated
- norm_biases_grad: float32 [3, 768], replicated
Inputs may be any that keep to these rules, and one draw needn't show every extreme that they name: `dec_starts`: each packed row holds 4 pairs; its offsets start at 0, rise strictly and stay below the row's used slots, so every decoder segment holds at least one used slot; padded slots belong to the last pair. `mem_starts`: pair j's table is memory segment j of the same packed row; offsets start at 0, rise strictly and stay below the row's used slots, so every memory segment holds at least one used slot.
All inputs are finite; a program needn't handle non-finite values.
Results may differ from a plain program's by a relative error of at most 0.023.
Values may be sent and summed in bfloat16 or wider, within the bound.
No kernel may reach another device: no remote copies, remote signals or barrier semaphores. Data moves between devices by JAX's collectives and lax.ppermute only.
A program may use at most 128 MiB of HBM per device.

v0:
```python
import jax
import jax.numpy as jnp
from jax import lax
from jax.sharding import PartitionSpec as P

HD = 64
NEG_FILL = -1000000000.0
EPSILON = 1e-05


def layer_norm(values, gain_row, bias_row):
    average = jnp.mean(values, -1, keepdims=True)
    centered = values - average
    variance = jnp.mean(centered * centered, -1, keepdims=True)
    return centered * lax.rsqrt(variance + EPSILON) * gain_row + bias_row


def exact_gelu(values):
    return jax.nn.gelu(values, approximate=False)


def segment_ids(starts, slot_count):
    places = jnp.arange(slot_count, dtype=jnp.int32)
    return jnp.sum((starts[:, None, :] <= places[None, :, None]).astype(jnp.int32), -1) - 1


def inner_dot(left_side, right_side):
    return lax.dot_general(
        left_side, right_side, (((0,), (0,)), ((), ())), preferred_element_type=jnp.float32
    )


def outer_dot(left_side, right_side):
    return lax.dot_general(
        left_side, right_side, (((1,), (1,)), ((), ())), preferred_element_type=jnp.float32
    )


def row_groups(kernel, arrays):
    row_count = arrays[0].shape[0]
    limit = max(1, 512 // arrays[0].shape[1])
    group_rows = max(
        (count for count in range(1, min(row_count, limit) + 1) if row_count % count == 0)
    )
    blocks = row_count // group_rows
    shaped = tuple((member.reshape((blocks, group_rows) + member.shape[1:]) for member in arrays))
    results = lax.map(lambda pieces: kernel(*pieces), shaped)
    return jax.tree.map(lambda member: member.reshape((row_count,) + member.shape[2:]), results)


def attend_block(queries, key_rows, value_rows, allowed):
    scores = jnp.einsum("rqhd,rkhd->rhqk", queries, key_rows, preferred_element_type=jnp.float32)
    scores = jnp.where(allowed[:, None], scores, NEG_FILL)
    peak_score = jnp.max(scores, -1, keepdims=True)
    weights = jnp.exp(scores - peak_score)
    totals = jnp.sum(weights, -1, keepdims=True)
    prob_low = (weights / totals).astype(jnp.bfloat16)
    output = jnp.einsum("rhqk,rkhd->rqhd", prob_low, value_rows, preferred_element_type=jnp.float32)
    return (output, (peak_score + jnp.log(totals))[..., 0])


def attend_back(queries, key_rows, value_rows, allowed, log_total, grad_rows):
    scores = jnp.einsum("rqhd,rkhd->rhqk", queries, key_rows, preferred_element_type=jnp.float32)
    scores = jnp.where(allowed[:, None], scores, NEG_FILL)
    prob_full = jnp.exp(scores - log_total[..., None])
    prob_low = prob_full.astype(jnp.bfloat16)
    value_grad = jnp.einsum(
        "rhqk,rqhd->rkhd", prob_low, grad_rows, preferred_element_type=jnp.float32
    )
    prob_grad = jnp.einsum(
        "rqhd,rkhd->rhqk", grad_rows, value_rows, preferred_element_type=jnp.float32
    )
    offset = jnp.sum(prob_full * prob_grad, -1, keepdims=True)
    score_grad = (prob_full * (prob_grad - offset)).astype(jnp.bfloat16)
    query_grad = jnp.einsum(
        "rhqk,rkhd->rqhd", score_grad, key_rows, preferred_element_type=jnp.float32
    )
    key_grad = jnp.einsum(
        "rhqk,rqhd->rkhd", score_grad, queries, preferred_element_type=jnp.float32
    )
    return (query_grad, key_grad, value_grad)


def body(
    hidden,
    memory,
    out_grad,
    dec_starts,
    dec_length,
    mem_starts,
    mem_length,
    self_qkv,
    self_qv_bias,
    self_proj,
    cross_query,
    cross_kv,
    cross_qv_bias,
    cross_proj,
    ffn_in,
    ffn_in_bias,
    ffn_out,
    out_biases,
    norm_gains,
    norm_biases,
):
    row_count = dec_starts.shape[0]
    dec_slots = hidden.shape[0] // row_count
    mem_slots = memory.shape[0] // row_count
    local_width = self_qkv.shape[2]
    head_count = local_width // HD
    scaling = HD ** (-0.5)
    dec_places = jnp.arange(dec_slots, dtype=jnp.int32)
    mem_places = jnp.arange(mem_slots, dtype=jnp.int32)
    dec_segment = segment_ids(dec_starts, dec_slots)
    mem_segment = segment_ids(mem_starts, mem_slots)
    self_allowed = (
        (dec_segment[:, :, None] == dec_segment[:, None, :])
        & (dec_places[None, None, :] <= dec_places[None, :, None])
        & (dec_places[None, None, :] < dec_length[:, None, None])
    )
    cross_allowed = (dec_segment[:, :, None] == mem_segment[:, None, :]) & (
        mem_places[None, None, :] < mem_length[:, None, None]
    )

    def split_heads(values):
        return values.reshape(row_count, values.shape[0] // row_count, head_count, HD)

    def merge_heads(values):
        return values.reshape(row_count * values.shape[1], local_width)

    self_weight = jnp.concatenate([self_qkv[0], self_qkv[1], self_qkv[2]], axis=1)
    projected = jnp.dot(hidden, self_weight, preferred_element_type=jnp.float32)
    self_q = split_heads(
        ((projected[:, :local_width] + self_qv_bias[0]) * scaling).astype(jnp.bfloat16)
    )
    self_k = split_heads(projected[:, local_width : 2 * local_width].astype(jnp.bfloat16))
    self_v = split_heads((projected[:, 2 * local_width :] + self_qv_bias[1]).astype(jnp.bfloat16))
    self_out, self_total = row_groups(attend_block, (self_q, self_k, self_v, self_allowed))
    self_low = merge_heads(self_out).astype(jnp.bfloat16)
    self_branch = lax.psum(jnp.dot(self_low, self_proj, preferred_element_type=jnp.float32), "mp")
    first, first_back = jax.vjp(
        layer_norm,
        hidden.astype(jnp.float32) + self_branch + out_biases[0],
        norm_gains[0],
        norm_biases[0],
    )
    first_low = first.astype(jnp.bfloat16)
    cross_pre = jnp.dot(first_low, cross_query, preferred_element_type=jnp.float32)
    cross_q = split_heads(((cross_pre + cross_qv_bias[0]) * scaling).astype(jnp.bfloat16))
    memory_whole = lax.all_gather(memory, "mp", axis=1, tiled=True)
    kv_weight = jnp.concatenate([cross_kv[0], cross_kv[1]], axis=1)
    memory_kv = jnp.dot(memory_whole, kv_weight, preferred_element_type=jnp.float32)
    cross_k = split_heads(memory_kv[:, :local_width].astype(jnp.bfloat16))
    cross_v = split_heads((memory_kv[:, local_width:] + cross_qv_bias[1]).astype(jnp.bfloat16))
    cross_out, cross_total = row_groups(attend_block, (cross_q, cross_k, cross_v, cross_allowed))
    cross_low = merge_heads(cross_out).astype(jnp.bfloat16)
    cross_branch = lax.psum(
        jnp.dot(cross_low, cross_proj, preferred_element_type=jnp.float32), "mp"
    )
    second, second_back = jax.vjp(
        layer_norm, first + cross_branch + out_biases[1], norm_gains[1], norm_biases[1]
    )
    second_low = second.astype(jnp.bfloat16)
    hidden_pre = jnp.dot(second_low, ffn_in, preferred_element_type=jnp.float32) + ffn_in_bias
    activated, gelu_back = jax.vjp(exact_gelu, hidden_pre)
    activated_low = activated.astype(jnp.bfloat16)
    ffn_branch = lax.psum(jnp.dot(activated_low, ffn_out, preferred_element_type=jnp.float32), "mp")
    final_norm, third_back = jax.vjp(
        layer_norm, second + ffn_branch + out_biases[2], norm_gains[2], norm_biases[2]
    )
    third_grad, gain_three, shift_three = third_back(out_grad.astype(jnp.float32))
    third_low = third_grad.astype(jnp.bfloat16)
    ffn_out_grad = inner_dot(activated_low, third_low)
    ffn_bias_out = jnp.sum(third_grad, 0)
    (pre_grad,) = gelu_back(outer_dot(third_low, ffn_out))
    ffn_in_bias_grad = jnp.sum(pre_grad, 0)
    pre_low = pre_grad.astype(jnp.bfloat16)
    ffn_in_grad = inner_dot(second_low, pre_low)
    second_grad = third_grad + lax.psum(outer_dot(pre_low, ffn_in), "mp")
    cross_grad, gain_two, shift_two = second_back(second_grad)
    cross_grad_low = cross_grad.astype(jnp.bfloat16)
    cross_proj_grad = inner_dot(cross_low, cross_grad_low)
    cross_bias_out = jnp.sum(cross_grad, 0)
    cross_out_grad = split_heads(outer_dot(cross_grad_low, cross_proj).astype(jnp.bfloat16))
    cq_grad, ck_grad, cv_grad = row_groups(
        attend_back, (cross_q, cross_k, cross_v, cross_allowed, cross_total, cross_out_grad)
    )
    cq_grad = merge_heads(cq_grad) * scaling
    cv_grad = merge_heads(cv_grad)
    cross_qv_grad = jnp.stack([jnp.sum(cq_grad, 0), jnp.sum(cv_grad, 0)])
    cq_low = cq_grad.astype(jnp.bfloat16)
    cross_query_grad = inner_dot(first_low, cq_low)
    first_grad = cross_grad + lax.psum(outer_dot(cq_low, cross_query), "mp")
    kv_grad_low = jnp.concatenate([merge_heads(ck_grad), cv_grad], axis=1).astype(jnp.bfloat16)
    kv_weight_grad = inner_dot(memory_whole, kv_grad_low)
    cross_kv_grad = jnp.stack([kv_weight_grad[:, :local_width], kv_weight_grad[:, local_width:]])
    memory_grad = lax.psum_scatter(
        outer_dot(kv_grad_low, kv_weight).astype(jnp.bfloat16),
        "mp",
        scatter_dimension=1,
        tiled=True,
    ).astype(jnp.float32)
    self_grad, gain_one, shift_one = first_back(first_grad)
    self_grad_low = self_grad.astype(jnp.bfloat16)
    self_proj_grad = inner_dot(self_low, self_grad_low)
    self_bias_out = jnp.sum(self_grad, 0)
    self_out_grad = split_heads(outer_dot(self_grad_low, self_proj).astype(jnp.bfloat16))
    sq_grad, sk_grad, sv_grad = row_groups(
        attend_back, (self_q, self_k, self_v, self_allowed, self_total, self_out_grad)
    )
    sq_grad = merge_heads(sq_grad) * scaling
    sv_grad = merge_heads(sv_grad)
    self_qv_grad = jnp.stack([jnp.sum(sq_grad, 0), jnp.sum(sv_grad, 0)])
    qkv_low = jnp.concatenate([sq_grad, merge_heads(sk_grad), sv_grad], axis=1).astype(jnp.bfloat16)
    qkv_weight_grad = inner_dot(hidden, qkv_low)
    self_qkv_grad = jnp.stack(
        [
            qkv_weight_grad[:, :local_width],
            qkv_weight_grad[:, local_width : 2 * local_width],
            qkv_weight_grad[:, 2 * local_width :],
        ]
    )
    hidden_grad = self_grad + lax.psum(
        outer_dot(qkv_low, self_weight).astype(jnp.bfloat16), "mp"
    ).astype(jnp.float32)
    (
        self_qkv_grad,
        self_qv_grad,
        self_proj_grad,
        cross_query_grad,
        cross_kv_grad,
        cross_qv_grad,
        cross_proj_grad,
        ffn_in_grad,
        ffn_in_bias_grad,
        ffn_out_grad,
        self_bias_out,
        cross_bias_out,
        ffn_bias_out,
        gain_one,
        gain_two,
        gain_three,
        shift_one,
        shift_two,
        shift_three,
    ) = lax.psum(
        (
            self_qkv_grad,
            self_qv_grad,
            self_proj_grad,
            cross_query_grad,
            cross_kv_grad,
            cross_qv_grad,
            cross_proj_grad,
            ffn_in_grad,
            ffn_in_bias_grad,
            ffn_out_grad,
            self_bias_out,
            cross_bias_out,
            ffn_bias_out,
            gain_one,
            gain_two,
            gain_three,
            shift_one,
            shift_two,
            shift_three,
        ),
        "dp",
    )
    out_biases_grad = jnp.stack([self_bias_out, cross_bias_out, ffn_bias_out])
    norm_gains_grad = jnp.stack([gain_one, gain_two, gain_three])
    norm_biases_grad = jnp.stack([shift_one, shift_two, shift_three])
    return (
        final_norm.astype(jnp.bfloat16),
        hidden_grad,
        memory_grad,
        self_qkv_grad,
        self_qv_grad,
        self_proj_grad,
        cross_query_grad,
        cross_kv_grad,
        cross_qv_grad,
        cross_proj_grad,
        ffn_in_grad,
        ffn_in_bias_grad,
        ffn_out_grad,
        out_biases_grad,
        norm_gains_grad,
        norm_biases_grad,
    )


def solution(mesh):
    placed = (
        P("dp", None),
        P("dp", "mp"),
        P("dp", None),
        P("dp", None),
        P("dp"),
        P("dp", None),
        P("dp"),
        P(None, None, "mp"),
        P(None, "mp"),
        P("mp", None),
        P(None, "mp"),
        P(None, None, "mp"),
        P(None, "mp"),
        P("mp", None),
        P(None, "mp"),
        P("mp"),
        P("mp", None),
        P(),
        P(),
        P(),
    )
    return jax.shard_map(
        body,
        mesh=mesh,
        in_specs=placed,
        out_specs=(
            P("dp", None),
            P("dp", None),
            P("dp", "mp"),
            P(None, None, "mp"),
            P(None, "mp"),
            P("mp", None),
            P(None, "mp"),
            P(None, None, "mp"),
            P(None, "mp"),
            P("mp", None),
            P(None, "mp"),
            P("mp"),
            P("mp", None),
            P(),
            P(),
            P(),
        ),
        check_vma=False,
    )
```

profile of v0, /device:TPU:0, one launch (start us, length us, event | category | flops | bytes accessed | tf_op | source)
XLA Modules:
  0.0 875.1 jit_solution(11104530872102401639)
XLA Ops:
  17.6 69.4 %all-reduce.10.cloned.1.call-done = f32[512,768]{1,0:T(8,128)} async-done(((f32[512,768]{1,0:T(8,128)}), f32[512,768]{1,0:T(8,128)}) %all-reduce.10.cloned.1.call-update) | async-done | bytes 1572880 | tf_op jit(solution)/shard_map/psum | solution.py:140
  92.5 110.5 %all-gather.2.cloned.1.call-done = bf16[4096,768]{0,1:T(8,128)(2,1)} async-done(((bf16[4096,192]{0,1:T(8,128)(2,1)}), bf16[4096,768]{0,1:T(8,128)(2,1)}) %all-gather.2.cloned.1.call-update) | async-done | bytes 6291472 | tf_op jit(solution)/shard_map/all_gather | solution.py:150
  203.0 4.8 convolution_bitcast_fusion
  211.8 3.9 squeeze.90
  215.7 3.4 fusion.4
  219.0 3.9 squeeze.88
  222.9 3.5 select_reduce_fusion
  233.8 67.3 %all-reduce.12.cloned.1.call-done = f32[512,768]{1,0:T(8,128)} async-done(((f32[512,768]{1,0:T(8,128)}), f32[512,768]{1,0:T(8,128)}) %all-reduce.12.cloned.1.call-update) | async-done | bytes 1572880 | tf_op jit(solution)/shard_map/psum | solution.py:157
  303.8 5.4 multiply_convert_fusion.1
  312.1 68.3 %all-reduce.14.cloned.1.call-done = f32[512,768]{1,0:T(8,128)} async-done(((f32[512,768]{1,0:T(8,128)}), f32[512,768]{1,0:T(8,128)}) %all-reduce.14.cloned.1.call-update) | async-done | bytes 1572880 | tf_op jit(solution)/shard_map/psum | solution.py:167
  391.6 68.2 %all-reduce.16.cloned.1.call-done = f32[512,768]{1,0:T(8,128)} async-done(((f32[512,768]{1,0:T(8,128)}), f32[512,768]{1,0:T(8,128)}) %all-reduce.16.cloned.1.call-update) | async-done | bytes 1572880 | tf_op jit(solution)/shard_map/psum | solution.py:179
  459.8 2.8 multiply_reduce_fusion.1
  465.0 6.5 multiply_reduce_fusion
  482.0 3.1 bitcast_convert_fusion
  489.5 56.1 %all-reduce.18.cloned.1.call-done = f32[512,768]{1,0:T(8,128)} async-done(((f32[512,768]{1,0:T(8,128)}), f32[512,768]{1,0:T(8,128)}) %all-reduce.18.cloned.1.call-update) | async-done | bytes 1572880 | tf_op jit(solution)/shard_map/psum | solution.py:193
  556.6 7.2 convolution_convert_fusion
  565.0 3.8 fusion.93
  571.2 5.5 convolution_bitcast_fusion.3
  587.4 10.8 %all-reduce.20.cloned.1.call-done = bf16[512,768]{1,0:T(8,128)(2,1)} async-done(((bf16[512,768]{1,0:T(8,128)(2,1)}), bf16[512,768]{1,0:T(8,128)(2,1)}) %all-reduce.20.cloned.1.call-update) | async-done | bytes 786448 | tf_op jit(solution)/shard_map/psum | solution.py:223
  600.8 25.6 %all-reduce = (f32[2,192]{1,0:T(2,128)}, f32[2,192]{1,0:T(2,128)}, f32[768]{0:T(1024)}, f32[1,768]{1,0:T(1,128)S(1)}, f32[1,768]{1,0:T(1,128)S(1)}, /*index=5*/f...) all-reduce(f32[2,192]{1,0:T(2,128)S(1)} %pad_maximum_fusion.11, ...), channel_id=1, replica_groups=mesh['dp'=8,'mp'=4] {'dp'}, use_global_device_ids=true, to_apply=%region_30.31 | all-reduce | flops 8448 | bytes 67584 | tf_op jit(solution)/shard_map/psum | solution.py:246
  628.2 82.3 %reduce-scatter.2.cloned.1.call-done = bf16[4096,192]{0,1:T(8,128)(2,1)} async-done(((bf16[4096,768]{0,1:T(8,128)(2,1)}), bf16[4096,192]{0,1:T(8,128)(2,1)}) %reduce-scatter.2.cloned.1.call-update) | async-done | bytes 1572880 | tf_op jit(solution)/shard_map/reduce_scatter | solution.py:197
  710.5 3.4 convert_element_type.157
  714.0 143.3 %all-reduce.22.cloned.1.call-done = (f32[3,768,192]{1,2,0:T(8,128)}, f32[192,768]{1,0:T(8,128)}, f32[768,192]{0,1:T(8,128)}, f32[2,768,192]{1,2,0:T(8,128)}, f32...) async-done(((f32[3,768,192]{1,2,0:T(8,128)}, f32[192,768]{1,0:T(8,128)}, f32[768,192]{0,1:T(8,128)}, f32[2,768,192]{1,2,0:T(8,128)}, f32[192,768]{1,0:T(8,128)}, ...) | async-done | bytes 9437200 | tf_op jit(solution)/shard_map/psum | solution.py:246
  857.3 2.9 copy.229
  (316 shorter events, 97.9 us)
Async XLA Ops:
  7.2 296.3 %copy-start = (bf16[768,768]{1,0:T(8,128)(2,1)S(1)}, bf16[768,768]{1,0:T(8,128)(2,1)}, u32[]{:S(2)}) copy-start(bf16[768,768]{1,0:T(8,128)(2,1)} %param.34) | copy-start | bytes 3538948
  7.2 79.8 %all-reduce.10.cloned.1.call-start = ((), (), s32[]{:S(2)}) async-start(), calls=%async_computation.1 | async-start | bytes 3145728 | tf_op jit(solution)/shard_map/psum | solution.py:140
  15.0 188.0 %all-gather.2.cloned.1.call-start = ((), (), s32[]{:S(2)}) async-start(), calls=%async_computation.2 | async-start | bytes 7864320 | tf_op jit(solution)/shard_map/all_gather | solution.py:150
  15.8 285.3 %all-reduce.12.cloned.1.call-start = ((), (), s32[]{:S(2)}) async-start(), calls=%async_computation.3 | async-start | bytes 3145728 | tf_op jit(solution)/shard_map/psum | solution.py:157
  16.1 364.2 %copy-start.63 = (f32[768]{0:T(1024)}, f32[768]{0:T(1024)S(1)}, u32[]{:S(2)}) copy-start(f32[768]{0:T(1024)S(1)} %get-tuple-element.122) | copy-start | bytes 9220
  16.7 211.4 %copy-start.12 = (pred[4,128,1024]{2,1,0:T(8,128)(4,1)}, pred[4,128,1024]{2,1,0:T(8,128)(4,1)S(1)}, u32[]{:S(2)}) copy-start(pred[4,128,1024]{2,1,0:T(8,128)(4,1)S(1)} %compare_and_fusion) | copy-start | bytes 1572868
  88.9 212.2 %copy-start.3 = (f32[512,768]{1,0:T(8,128)}, f32[512,768]{1,0:T(8,128)S(1)}, u32[]{:S(2)}) copy-start(f32[512,768]{1,0:T(8,128)S(1)} %get-tuple-element.170) | copy-start | bytes 4718596
  233.6 146.7 %all-reduce.14.cloned.1.call-start = ((), (), s32[]{:S(2)}) async-start(), calls=%async_computation.4 | async-start | bytes 3145728 | tf_op jit(solution)/shard_map/psum | solution.py:167
  303.1 6.1 copy-start.5
  303.8 6.3 copy-start.74
  312.0 68.3 %copy-start.6 = (f32[512,768]{1,0:T(8,128)S(1)}, f32[512,768]{1,0:T(8,128)}, u32[]{:S(2)}) copy-start(f32[512,768]{1,0:T(8,128)} %copy-done.5) | copy-start | bytes 4718596
  312.0 147.8 %all-reduce.16.cloned.1.call-start = ((), (), s32[]{:S(2)}) async-start(), calls=%async_computation.5 | async-start | bytes 3145728 | tf_op jit(solution)/shard_map/psum | solution.py:179
  391.5 154.1 %all-reduce.18.cloned.1.call-start = ((), (), s32[]{:S(2)}) async-start(), calls=%async_computation.6 | async-start | bytes 3145728 | tf_op jit(solution)/shard_map/psum | solution.py:193
  465.0 6.5 slice-start
  465.0 6.5 slice-start.1
  477.2 4.8 slice-start.2
  477.2 121.0 %all-reduce.20.cloned.1.call-start = ((), (), s32[]{:S(2)}) async-start(), calls=%async_computation.7 | async-start | bytes 1572864 | tf_op jit(solution)/shard_map/psum | solution.py:223
  477.5 4.5 slice-start.3
  488.2 57.4 %copy-start.4 = (f32[512,768]{1,0:T(8,128)S(1)}, f32[512,768]{1,0:T(8,128)}, u32[]{:S(2)}) copy-start(f32[512,768]{1,0:T(8,128)} %copy-done.3) | copy-start | bytes 4718596
  555.3 155.2 %reduce-scatter.2.cloned.1.call-start = ((), (), s32[]{:S(2)}) async-start(), calls=%async_computation.8 | async-start | bytes 7864320 | tf_op jit(solution)/shard_map/reduce_scatter | solution.py:197
  563.9 4.9 copy-start.7
  563.9 4.9 copy-start.64
  563.9 293.4 %all-reduce.22.cloned.1.call-start = ((), (), s32[]{:S(2)}) async-start(), calls=%async_computation.9 | async-start | bytes 18874368 | tf_op jit(solution)/shard_map/psum | solution.py:246
  587.4 13.4 %copy-start.68 = (f32[768]{0:T(1024)S(1)}, f32[768]{0:T(1024)}, u32[]{:S(2)}) copy-start(f32[768]{0:T(1024)} %get-tuple-element.210) | copy-start | bytes 9220
  (71 other events, 118.6 us)
Sparse Core Ops, SparseCore 0:
  15.2 71.7 all-reduce.9
  88.6 114.3 all-gather.1
  233.7 67.3 all-reduce.11
  312.2 68.1 all-reduce.13
  391.6 68.1 all-reduce.15
  477.4 68.1 all-reduce.17
  555.4 42.7 all-reduce.19
  600.5 109.9 reduce-scatter.1
  716.5 140.7 all-reduce.21
where the time goes:
time: 884 us; the launch traced here: 875 us
  waiting for transfers between devices  677 us (77%)
  matrix products  70.8 us (8%)
  local copies, waits for them, and re-layouts  47.4 us (5%)
  other arithmetic  37.7 us (4%)
  blocking collectives  25.6 us (3%)
  between operations  15.5 us (2%)
    psum x1, waiting for transfers between devices, body(): lax.psum((self_qkv_grad, self_qv_grad, self_proj_grad, cross_query_grad,...  143 us
    all_gather x1, waiting for transfers between devices, body(): memory_whole = lax.all_gather(memory, 'mp', axis=1, tiled=True)  110 us
    reduce_scatter x1, waiting for transfers between devices, body(): lax.psum_scatter(outer_dot(kv_grad_low, kv_weight).astype(jnp.bfloat16),...  82.3 us
    psum x1, waiting for transfers between devices, body(): lax.psum(jnp.dot(self_low, self_proj, preferred_element_type=jnp.float32)...  69.4 us
    psum x1, waiting for transfers between devices, body(): lax.psum(jnp.dot(activated_low, ffn_out, preferred_element_type=jnp.float...  68.3 us
    psum x1, waiting for transfers between devices, body(): second_grad = third_grad + lax.psum(outer_dot(pre_low, ffn_in), 'mp')  68.2 us
    psum x1, waiting for transfers between devices, body(): lax.psum(jnp.dot(cross_low, cross_proj, preferred_element_type=jnp.float3...  67.3 us
    psum x1, waiting for transfers between devices, body(): first_grad = cross_grad + lax.psum(outer_dot(cq_low, cross_query), 'mp')  56.1 us
  transfers between devices with their start and end apart: 9, of which 9 were waited for; matrix products, arithmetic and copies ran while one was open for 6% of the time, Pallas kernels for 0%

commit v1 on v0

--- a/solution.py
+++ b/solution.py
@@ -147,7 +147,22 @@
     first_low = first.astype(jnp.bfloat16)
     cross_pre = jnp.dot(first_low, cross_query, preferred_element_type=jnp.float32)
     cross_q = split_heads(((cross_pre + cross_qv_bias[0]) * scaling).astype(jnp.bfloat16))
-    memory_whole = lax.all_gather(memory, "mp", axis=1, tiled=True)
+    devices, here, rows = (lax.axis_size("mp"), lax.axis_index("mp"), memory.shape[1])
+    forward = [(i, (i + 1) % devices) for i in range(devices)]
+    behind = [(i, (i - 1) % devices) for i in range(devices)]
+    out = jnp.zeros((*memory.shape[:1], devices * rows, *memory.shape[1 + 1 :]), memory.dtype)
+    out = lax.dynamic_update_slice_in_dim(out, memory, here * rows, axis=1)
+    from_left = from_right = memory
+    half = devices // 2
+    for lap in range(1, half + 1):
+        from_left = lax.ppermute(from_left, "mp", forward)
+        out = lax.dynamic_update_slice_in_dim(out, from_left, (here - lap) % devices * rows, axis=1)
+        if lap < devices - half:
+            from_right = lax.ppermute(from_right, "mp", behind)
+            out = lax.dynamic_update_slice_in_dim(
+                out, from_right, (here + lap) % devices * rows, axis=1
+            )
+    memory_whole = out
     kv_weight = jnp.concatenate([cross_kv[0], cross_kv[1]], axis=1)
     memory_kv = jnp.dot(memory_whole, kv_weight, preferred_element_type=jnp.float32)
     cross_k = split_heads(memory_kv[:, :local_width].astype(jnp.bfloat16))

time: 884 us -> 855 us (0.967)
  waiting for transfers between devices: 677 us -> 595 us
  starting transfers between devices: 1.01 us -> 45.1 us
  local copies, waits for them, and re-layouts: 47.4 us -> 60.3 us
    all_gather x1 -> x0, waiting for transfers between devices: 110 us -> none  [body(): memory_whole = lax.all_gather(memory, 'mp', axis=1, tiled=True)]
    ppermute x0 -> x3, starting transfers between devices: none -> 44.1 us  [the longest x2 42 us: body(): from_left = lax.ppermute(from_left, 'mp', forward)]
    ppermute x0 -> x3, waiting for transfers between devices: none -> 39.8 us  [the longest x2 39.8 us: body(): from_left = lax.ppermute(from_left, 'mp', forward)]
    psum x1, waiting for transfers between devices: 69.4 us -> 58.7 us  [body(): lax.psum(jnp.dot(self_low, self_proj, preferred_element_type=jnp.float32)...]
    dynamic_update_slice x0 -> x4, local copies, waits for them, and re-layouts: none -> 9.47 us  [the longest x2 5.51 us: body(): lax.dynamic_update_slice_in_dim(out, from_left, (here - lap) % devices *...]
    unnamed x184 -> x190, local copies, waits for them, and re-layouts: 29.7 us -> 29.6 us
  transfers between devices with their start and end apart: 9 -> 11, of which waited for: 9 -> 9; matrix products, arithmetic and copies ran while one was open for 6% -> 8% of each run, Pallas kernels for 0% -> 0%
where the time goes in v1:
time: 855 us; the launch traced here: 850 us
  waiting for transfers between devices  595 us (70%)
  matrix products  71 us (8%)
  local copies, waits for them, and re-layouts  60.3 us (7%)
  starting transfers between devices  45.1 us (5%)
  other arithmetic  37.6 us (4%)
  blocking collectives  25.6 us (3%)
  between operations  15.6 us (2%)
    psum x1, waiting for transfers between devices, body(): lax.psum((self_qkv_grad, self_qv_grad, self_proj_grad, cross_query_grad,...  143 us
    reduce_scatter x1, waiting for transfers between devices, body(): lax.psum_scatter(outer_dot(kv_grad_low, kv_weight).astype(jnp.bfloat16),...  82.4 us
    psum x1, waiting for transfers between devices, body(): second_grad = third_grad + lax.psum(outer_dot(pre_low, ffn_in), 'mp')  68.2 us
    psum x1, waiting for transfers between devices, body(): lax.psum(jnp.dot(activated_low, ffn_out, preferred_element_type=jnp.float...  68.1 us
    psum x1, waiting for transfers between devices, body(): lax.psum(jnp.dot(cross_low, cross_proj, preferred_element_type=jnp.float3...  67.5 us
    psum x1, waiting for transfers between devices, body(): lax.psum(jnp.dot(self_low, self_proj, preferred_element_type=jnp.float32)...  58.7 us
    psum x1, waiting for transfers between devices, body(): first_grad = cross_grad + lax.psum(outer_dot(cq_low, cross_query), 'mp')  56.1 us
    ppermute x2, starting transfers between devices, body(): from_left = lax.ppermute(from_left, 'mp', forward)  42 us
  transfers between devices with their start and end apart: 11, of which 9 were waited for; matrix products, arithmetic and copies ran while one was open for 8% of the time, Pallas kernels for 0%

profile of v1, /device:TPU:0, one launch (start us, length us, event | category | flops | bytes accessed | tf_op | source)
XLA Modules:
  0.0 850.0 jit_solution(8673292777087268438)
XLA Ops:
  22.0 3.4 broadcast_in_dim.139
  26.7 39.8 %collective-permute-done = bf16[4096,192]{0,1:T(8,128)(2,1)} collective-permute-done((bf16[4096,192]{0,1:T(8,128)(2,1)}, bf16[4096,192]{0,1:T(8,128)(2,1)}, u32[]{:S(2)}, u32[]{:S(2)}) %collective-permute-start) | collective-permute-done | bytes 1572896 | tf_op jit(solution)/shard_map/ppermute | solution.py:158
  66.6 39.0 %collective-permute-start.2 = (bf16[4096,192]{0,1:T(8,128)(2,1)}, bf16[4096,192]{0,1:T(8,128)(2,1)}, u32[]{:S(2)}, u32[]{:S(2)}) collective-permute-start(bf16[4096,192]{0,1:T(8,128)(2,1)} %collective-permute-done), channel_id=1, source_target_pairs={{0,1},{1,2},{2,3},{3,0},{4,5},{5,6},{6,7},{7,4},{8,9},{9,10},{10,1... | collective-permute-start | bytes 4718600 | tf_op jit(solution)/shard_map/ppermute | solution.py:158
  105.5 58.7 %all-reduce.10.cloned.1.call-done = f32[512,768]{1,0:T(8,128)} async-done(((f32[512,768]{1,0:T(8,128)}), f32[512,768]{1,0:T(8,128)}) %all-reduce.10.cloned.1.call-update) | async-done | bytes 1572880 | tf_op jit(solution)/shard_map/psum | solution.py:140
  177.9 4.7 fusion.53
  186.6 3.9 squeeze.90
  190.5 3.4 fusion.4
  193.8 3.9 squeeze.88
  197.7 3.5 select_reduce_fusion
  208.5 67.5 %all-reduce.12.cloned.1.call-done = f32[512,768]{1,0:T(8,128)} async-done(((f32[512,768]{1,0:T(8,128)}), f32[512,768]{1,0:T(8,128)}) %all-reduce.12.cloned.1.call-update) | async-done | bytes 1572880 | tf_op jit(solution)/shard_map/psum | solution.py:172
  278.7 5.4 multiply_convert_fusion.1
  287.1 68.1 %all-reduce.14.cloned.1.call-done = f32[512,768]{1,0:T(8,128)} async-done(((f32[512,768]{1,0:T(8,128)}), f32[512,768]{1,0:T(8,128)}) %all-reduce.14.cloned.1.call-update) | async-done | bytes 1572880 | tf_op jit(solution)/shard_map/psum | solution.py:182
  366.4 68.2 %all-reduce.16.cloned.1.call-done = f32[512,768]{1,0:T(8,128)} async-done(((f32[512,768]{1,0:T(8,128)}), f32[512,768]{1,0:T(8,128)}) %all-reduce.16.cloned.1.call-update) | async-done | bytes 1572880 | tf_op jit(solution)/shard_map/psum | solution.py:194
  439.8 6.5 multiply_reduce_fusion
  456.8 3.2 bitcast_convert_fusion
  464.2 56.1 %all-reduce.18.cloned.1.call-done = f32[512,768]{1,0:T(8,128)} async-done(((f32[512,768]{1,0:T(8,128)}), f32[512,768]{1,0:T(8,128)}) %all-reduce.18.cloned.1.call-update) | async-done | bytes 1572880 | tf_op jit(solution)/shard_map/psum | solution.py:208
  531.4 7.2 convolution_convert_fusion
  539.8 3.8 fusion.94
  546.0 5.6 fusion.117
  562.4 10.5 %all-reduce.20.cloned.1.call-done = bf16[512,768]{1,0:T(8,128)(2,1)} async-done(((bf16[512,768]{1,0:T(8,128)(2,1)}), bf16[512,768]{1,0:T(8,128)(2,1)}) %all-reduce.20.cloned.1.call-update) | async-done | bytes 786448 | tf_op jit(solution)/shard_map/psum | solution.py:238
  575.5 25.6 %all-reduce = (f32[2,192]{1,0:T(2,128)}, f32[2,192]{1,0:T(2,128)}, f32[768]{0:T(1024)}, f32[1,768]{1,0:T(1,128)S(1)}, f32[1,768]{1,0:T(1,128)S(1)}, /*index=5*/f...) all-reduce(f32[2,192]{1,0:T(2,128)S(1)} %pad_maximum_fusion.11, ...), channel_id=1, replica_groups=mesh['dp'=8,'mp'=4] {'dp'}, use_global_device_ids=true, to_apply=%region_30.31 | all-reduce | flops 8448 | bytes 67584 | tf_op jit(solution)/shard_map/psum | solution.py:261
  602.9 82.4 %reduce-scatter.2.cloned.1.call-done = bf16[4096,192]{0,1:T(8,128)(2,1)} async-done(((bf16[4096,768]{0,1:T(8,128)(2,1)}), bf16[4096,192]{0,1:T(8,128)(2,1)}) %reduce-scatter.2.cloned.1.call-update) | async-done | bytes 1572880 | tf_op jit(solution)/shard_map/reduce_scatter | solution.py:212
  685.3 3.4 convert_element_type.157
  688.7 143.3 %all-reduce.22.cloned.1.call-done = (f32[3,768,192]{1,2,0:T(8,128)}, f32[192,768]{1,0:T(8,128)}, f32[768,192]{0,1:T(8,128)}, f32[2,768,192]{1,2,0:T(8,128)}, f32...) async-done(((f32[3,768,192]{1,2,0:T(8,128)}, f32[192,768]{1,0:T(8,128)}, f32[768,192]{0,1:T(8,128)}, f32[2,768,192]{1,2,0:T(8,128)}, f32[192,768]{1,0:T(8,128)}, ...) | async-done | bytes 9437200 | tf_op jit(solution)/shard_map/psum | solution.py:261
  (330 shorter events, 117.3 us)
Async XLA Ops:
  7.2 271.1 %copy-start = (bf16[768,768]{1,0:T(8,128)(2,1)S(1)}, bf16[768,768]{1,0:T(8,128)(2,1)}, u32[]{:S(2)}) copy-start(bf16[768,768]{1,0:T(8,128)(2,1)} %param.34) | copy-start | bytes 3538948
  7.2 7.3 copy-start.25
  7.2 157.0 %all-reduce.10.cloned.1.call-start = ((), (), s32[]{:S(2)}) async-start(), calls=%async_computation.1 | async-start | bytes 3145728 | tf_op jit(solution)/shard_map/psum | solution.py:140
  7.3 59.3 %collective-permute-start = (bf16[4096,192]{0,1:T(8,128)(2,1)}, bf16[4096,192]{0,1:T(8,128)(2,1)}, u32[]{:S(2)}, u32[]{:S(2)}) collective-permute-start(bf16[4096,192]{0,1:T(8,128)(2,1)} %param.21), channel_id=1, source_target_pairs={{0,1},{1,2},{2,3},{3,0},{4,5},{5,6},{6,7},{7,4},{8,9},{9,10},{10,1... | collective-permute-start | bytes 4718600 | tf_op jit(solution)/shard_map/ppermute | solution.py:158
  10.3 162.1 %collective-permute-start.1 = (bf16[4096,192]{0,1:T(8,128)(2,1)}, bf16[4096,192]{0,1:T(8,128)(2,1)}, u32[]{:S(2)}, u32[]{:S(2)}) collective-permute-start(bf16[4096,192]{0,1:T(8,128)(2,1)} %param.21), channel_id=1, source_target_pairs={{0,3},{1,0},{2,1},{3,2},{4,7},{5,4},{6,5},{7,6},{8,11},{9,8},{10,9... | collective-permute-start | bytes 4718600 | tf_op jit(solution)/shard_map/ppermute | solution.py:161
  20.1 255.9 %all-reduce.12.cloned.1.call-start = ((), (), s32[]{:S(2)}) async-start(), calls=%async_computation.2 | async-start | bytes 3145728 | tf_op jit(solution)/shard_map/psum | solution.py:172
  20.5 334.8 %copy-start.66 = (f32[768]{0:T(1024)}, f32[768]{0:T(1024)S(1)}, u32[]{:S(2)}) copy-start(f32[768]{0:T(1024)S(1)} %get-tuple-element.122) | copy-start | bytes 9220
  21.1 181.8 %copy-start.12 = (pred[4,128,1024]{2,1,0:T(8,128)(4,1)}, pred[4,128,1024]{2,1,0:T(8,128)(4,1)S(1)}, u32[]{:S(2)}) copy-start(pred[4,128,1024]{2,1,0:T(8,128)(4,1)S(1)} %compare_and_fusion) | copy-start | bytes 1572868
  66.6 108.6 %collective-permute-start.2 = (bf16[4096,192]{0,1:T(8,128)(2,1)}, bf16[4096,192]{0,1:T(8,128)(2,1)}, u32[]{:S(2)}, u32[]{:S(2)}) collective-permute-start(bf16[4096,192]{0,1:T(8,128)(2,1)} %collective-permute-done), channel_id=1, source_target_pairs={{0,1},{1,2},{2,3},{3,0},{4,5},{5,6},{6,7},{7,4},{8,9},{9,10},{10,1... | collective-permute-start | bytes 4718600 | tf_op jit(solution)/shard_map/ppermute | solution.py:158
  166.1 109.9 %copy-start.3 = (f32[512,768]{1,0:T(8,128)}, f32[512,768]{1,0:T(8,128)S(1)}, u32[]{:S(2)}) copy-start(f32[512,768]{1,0:T(8,128)S(1)} %get-tuple-element.170) | copy-start | bytes 4718596
  208.4 146.8 %all-reduce.14.cloned.1.call-start = ((), (), s32[]{:S(2)}) async-start(), calls=%async_computation.3 | async-start | bytes 3145728 | tf_op jit(solution)/shard_map/psum | solution.py:182
  278.0 6.1 copy-start.5
  278.7 6.3 copy-start.77
  286.9 68.3 %copy-start.6 = (f32[512,768]{1,0:T(8,128)S(1)}, f32[512,768]{1,0:T(8,128)}, u32[]{:S(2)}) copy-start(f32[512,768]{1,0:T(8,128)} %copy-done.5) | copy-start | bytes 4718596
  286.9 147.7 %all-reduce.16.cloned.1.call-start = ((), (), s32[]{:S(2)}) async-start(), calls=%async_computation.4 | async-start | bytes 3145728 | tf_op jit(solution)/shard_map/psum | solution.py:194
  366.3 154.0 %all-reduce.18.cloned.1.call-start = ((), (), s32[]{:S(2)}) async-start(), calls=%async_computation.5 | async-start | bytes 3145728 | tf_op jit(solution)/shard_map/psum | solution.py:208
  439.7 6.5 slice-start
  439.8 6.5 slice-start.1
  452.0 120.9 %all-reduce.20.cloned.1.call-start = ((), (), s32[]{:S(2)}) async-start(), calls=%async_computation.6 | async-start | bytes 1572864 | tf_op jit(solution)/shard_map/psum | solution.py:238
  462.9 57.4 %copy-start.4 = (f32[512,768]{1,0:T(8,128)S(1)}, f32[512,768]{1,0:T(8,128)}, u32[]{:S(2)}) copy-start(f32[512,768]{1,0:T(8,128)} %copy-done.3) | copy-start | bytes 4718596
  530.1 155.3 %reduce-scatter.2.cloned.1.call-start = ((), (), s32[]{:S(2)}) async-start(), calls=%async_computation.7 | async-start | bytes 7864320 | tf_op jit(solution)/shard_map/reduce_scatter | solution.py:212
  538.7 4.9 copy-start.7
  538.7 293.4 %all-reduce.22.cloned.1.call-start = ((), (), s32[]{:S(2)}) async-start(), calls=%async_computation.8 | async-start | bytes 18874368 | tf_op jit(solution)/shard_map/psum | solution.py:261
  562.4 13.1 %copy-start.71 = (f32[768]{0:T(1024)S(1)}, f32[768]{0:T(1024)}, u32[]{:S(2)}) copy-start(f32[768]{0:T(1024)} %get-tuple-element.210) | copy-start | bytes 9220
  (76 other events, 143.7 us)
Sparse Core Ops, SparseCore 0:
  20.2 143.9 all-reduce.9
  208.5 67.3 all-reduce.11
  287.0 68.1 all-reduce.13
  366.5 68.1 all-reduce.15
  452.1 68.1 all-reduce.17
  530.2 42.6 all-reduce.19
  575.2 110.0 reduce-scatter.1
  691.2 140.7 all-reduce.21
